TPU v7x, 32 devices: a whole 2x2x4 slice. The times are simulated.
32 devices in a mesh: dp: 8 (over z, x), tensor: 4 (over y, core).
Axes of the slice: x: 2, y: 2, z: 4, core: 2. Of those that a mesh axis runs over, the one named last changes fastest.
Arguments:
- context: bfloat16 [2, 8192, 3072], P(None, 'dp', 'tensor'), may hold values from -6 to 6
- out_grad: bfloat16 [2, 8192, 3072], P(None, ('dp', 'tensor')), may hold values from -0.1875 to 0.1875
- error_in: bfloat16 [2, 24576, 3072], P(None, 'dp', 'tensor'), may hold values from -6 to 6
- right_init: float32 [2, 64, 3072], P(None, None, 'tensor'), may hold values from -6 to 6
Outputs:
- summed_update: bfloat16 [2, 3072, 3072], P(None, 'dp', 'tensor')
- error_out: bfloat16 [2, 24576, 3072], P(None, 'dp', 'tensor')
All inputs are finite; a program needn't handle non-finite values.
Results may differ from a plain program's by a relative error of at most 0.015.
Values may be sent and summed in bfloat16 or wider, within the bound.
A program may use at most 128 MiB of HBM per device.

v0:
```python
import jax
import jax.numpy as jnp
from jax import lax
from jax.sharding import PartitionSpec as P


def solve_rows(gram_matrix, left_factor):
    ridge_term = 1e-06 * jnp.mean(jnp.diagonal(gram_matrix, axis1=1, axis2=2), axis=1)
    eye_matrix = jnp.eye(gram_matrix.shape[1], dtype=gram_matrix.dtype)
    gram_matrix = gram_matrix + ridge_term[:, None, None] * eye_matrix
    factor_low = jnp.linalg.cholesky(gram_matrix)

    def one_solve(low_part, rhs_part):
        return jax.scipy.linalg.solve_triangular(low_part, rhs_part, lower=True)

    return jax.vmap(one_solve)(factor_low, left_factor)


def gram_of(left_factor):
    return jnp.einsum("lrd,lsd->lrs", left_factor, left_factor, precision=lax.Precision.HIGHEST)


def compress(context, out_grad, error_in, right_init):
    out_width = out_grad.shape[2]
    moment = jnp.einsum(
        "ltd,lte->lde",
        lax.all_gather(out_grad, "tensor", axis=1, tiled=True),
        context,
        preferred_element_type=jnp.float32,
    )
    moment = moment + error_in.astype(jnp.float32)
    left_factor = jnp.einsum("lre,lde->lrd", right_init, moment, precision=lax.Precision.HIGHEST)
    left_part = lax.psum_scatter(left_factor, "tensor", scatter_dimension=2, tiled=True)
    left_part = lax.psum(left_part, "dp")
    gram_matrix = lax.psum(gram_of(left_part), "tensor")
    ortho_part = solve_rows(gram_matrix, left_part)
    ortho_basis = lax.all_gather(ortho_part, "tensor", axis=2, tiled=True)
    right_terms = jnp.einsum("lrd,lde->lre", ortho_basis, moment, precision=lax.Precision.HIGHEST)
    right_factor = lax.psum(right_terms.astype(jnp.bfloat16), "dp").astype(jnp.float32)
    replicas = lax.axis_size("dp")
    row_share = out_width // replicas
    own_basis = lax.dynamic_slice_in_dim(
        ortho_basis, lax.axis_index("dp") * row_share, row_share, 2
    )
    summed = jnp.einsum("lrd,lre->lde", own_basis, right_factor, precision=lax.Precision.HIGHEST)
    mean_part = jnp.einsum(
        "lrd,lre->lde", ortho_basis, right_factor / replicas, precision=lax.Precision.HIGHEST
    )
    new_error = (moment - mean_part).astype(jnp.bfloat16)
    return (summed.astype(jnp.bfloat16), new_error)


def body(context, out_grad, error_in, right_init):
    return compress(context, out_grad, error_in, right_init)


def solution(mesh):
    return jax.shard_map(
        body,
        mesh=mesh,
        in_specs=(
            P(None, "dp", "tensor"),
            P(None, ("dp", "tensor"), None),
            P(None, "dp", "tensor"),
            P(None, None, "tensor"),
        ),
        out_specs=(P(None, "dp", "tensor"), P(None, "dp", "tensor")),
        check_vma=False,
    )
```

profile of v0, /device:TPU:0, one launch (start us, length us, event | category | flops | bytes accessed | tf_op | source)
XLA Modules:
  0.0 419.1 jit_solution(9212171889300298580)
XLA Ops:
  7.2 4.8 %copy.12 = bf16[2,256,3072]{1,2,0:T(8,128)(2,1)} copy(bf16[2,256,3072]{2,1,0:T(8,128)(2,1)} %param.5) | data formatting | bytes 6291456 | tf_op args[1]
  12.1 86.6 %all-gather.3.cloned.1.call-done = bf16[2,1024,3072]{1,2,0:T(8,128)(2,1)} async-done(((bf16[2,256,3072]{1,2,0:T(8,128)(2,1)}), bf16[2,1024,3072]{1,2,0:T(8,128)(2,1)}) %all-gather.3.cloned.1.call-update) | async-done | bytes 12582928 | tf_op jit(solution)/shard_map/all_gather | solution.py:27
  98.7 19.3 %convert_add_fusion = f32[2,3072,768]{2,1,0:T(8,128)} fusion(bf16[2,3072,768]{2,1,0:T(8,128)(2,1)} %param.6, bf16[2,1024,3072]{1,2,0:T(8,128)(2,1)} %all-gather.3.cloned.1.call-done, bf16[2,1024,768]{2,1,0:T(8,128)(2,1)S(1)} %copy-done), kind=kOutput, calls=%fused_computation.2 | convolution fusion | flops 9673113600 | bytes 44040192 | tf_op jit(solution)/shard_map/ltd,lte->lde/dot_general | solution.py:25
  118.0 22.5 %convolution_bitcast_fusion = f32[2,64,3072]{2,1,0:T(8,128)} fusion(f32[2,3072,768]{2,1,0:T(8,128)} %convert_add_fusion, f32[2,64,768]{2,1,0:T(8,128)S(1)} %copy-done.4), kind=kOutput, calls=%fused_computation.3 | convolution fusion | flops 3623878656 | bytes 20840448 | tf_op jit(solution)/shard_map/lre,lde->lrd/dot_general | solution.py:32
  140.5 28.1 %reduce-scatter.2.cloned.1.call-done = f32[2,64,768]{2,1,0:T(8,128)} async-done(((f32[2,64,3072]{2,1,0:T(8,128)}), f32[2,64,768]{2,1,0:T(8,128)}) %reduce-scatter.2.cloned.1.call-update) | async-done | bytes 393232 | tf_op jit(solution)/shard_map/reduce_scatter | solution.py:33
  168.7 0.1 copy.15
  168.9 75.0 %all-reduce.3.cloned.1.call-done = f32[2,64,768]{2,1,0:T(8,128)} async-done(((f32[2,64,768]{2,1,0:T(8,128)}), f32[2,64,768]{2,1,0:T(8,128)}) %all-reduce.3.cloned.1.call-update) | async-done | bytes 393232 | tf_op jit(solution)/shard_map/psum | solution.py:34
  243.9 1.7 fusion.10
  245.5 10.9 %psum.22 = f32[2,64,64]{1,2,0:T(8,128)S(1)} all-reduce(f32[2,64,64]{1,2,0:T(8,128)S(1)} %fusion.10), channel_id=1, replica_groups=mesh['dp'=8,'tensor'=4] {'tensor'}, use_global_device_ids=true, to_apply=%region_2.0 | all-reduce | flops 8192 | bytes 65536 | tf_op jit(solution)/shard_map/psum | solution.py:35
  256.4 1.9 copy.14
  258.3 0.9 gather_fusion
  259.3 0.1 multiply_add_fusion
  259.3 0.1 copy.16
  259.4 0.1 fusion.6
  259.5 11.7 %custom-call.8 = f32[2,64,64]{2,1,0:T(8,128)S(1)} custom-call(f32[2,64,64]{2,1,0:T(8,128)S(1)} %fusion.6), custom_call_target="Cholesky" | custom-call | tf_op jit(solution)/shard_map/jit(cholesky)/cholesky | solution.py:11
  271.3 0.1 compare_reduce_fusion
  271.4 0.1 select_bitcast_fusion
  271.5 9.8 %custom-call.9 = f32[2,1,64,64]{2,3,1,0:T(8,128)S(1)} custom-call(f32[2,1,64,64]{3,2,1,0:T(8,128)S(1)} %select_bitcast_fusion), custom_call_target="InvertDiagBlocksLowerTriangular" | custom-call | tf_op jit(solution)/shard_map/vmap(jit(_solve_triangular))/triangular_solve | solution.py:14
  281.3 1.3 fusion.4
  282.7 18.8 %all-gather.5.cloned.1.call-done = f32[2,64,3072]{2,1,0:T(8,128)} async-done(((f32[2,64,768]{2,1,0:T(8,128)}), f32[2,64,3072]{2,1,0:T(8,128)}) %all-gather.5.cloned.1.call-update) | async-done | bytes 1572880 | tf_op jit(solution)/shard_map/all_gather | solution.py:37
  301.5 16.3 %convolution_convert_fusion.1 = bf16[2,64,768]{2,1,0:T(8,128)(2,1)} fusion(f32[2,64,3072]{2,1,0:T(8,128)} %all-gather.5.cloned.1.call-done, f32[2,3072,768]{2,1,0:T(8,128)} %convert_add_fusion), kind=kOutput, calls=%fused_computation.5 | convolution fusion | flops 3623976960 | bytes 20643840 | tf_op jit(solution)/shard_map/lrd,lde->lre/dot_general | solution.py:38
  317.8 70.8 %all-reduce.5.cloned.1.call-done = bf16[2,64,768]{2,1,0:T(8,128)(2,1)} async-done(((bf16[2,64,768]{2,1,0:T(8,128)(2,1)}), bf16[2,64,768]{2,1,0:T(8,128)(2,1)}) %all-reduce.5.cloned.1.call-update) | async-done | bytes 196624 | tf_op jit(solution)/shard_map/psum | solution.py:39
  388.6 20.9 %subtract_convert_fusion = bf16[2,3072,768]{2,1,0:T(8,128)(2,1)} fusion(f32[2,3072,768]{2,1,0:T(8,128)} %convert_add_fusion, f32[2,64,3072]{2,1,0:T(8,128)} %all-gather.5.cloned.1.call-done, bf16[2,64,768]{2,1,0:T(8,128)(2,1)} %all-reduce.5.cloned.1.call-done), kind=kOutput, calls=%fused_computation.1 | convolution fusion | flops 3633512448 | bytes 30081024 | tf_op jit(solution)/shard_map/lrd,lre->lde/dot_general | solution.py:46
  409.5 3.1 convolution_convert_fusion
  (27 shorter events, 0.4 us)
Async XLA Ops:
  7.2 91.5 %copy-start = (bf16[2,1024,768]{2,1,0:T(8,128)(2,1)S(1)}, bf16[2,1024,768]{2,1,0:T(8,128)(2,1)}, u32[]{:S(2)}) copy-start(bf16[2,1024,768]{2,1,0:T(8,128)(2,1)} %param.4) | copy-start | bytes 9437188
  7.2 91.5 %all-gather.3.cloned.1.call-start = ((), (), s32[]{:S(2)}) async-start(), calls=%async_computation.1 | async-start | bytes 15728640 | tf_op jit(solution)/shard_map/all_gather | solution.py:27
  12.0 105.9 %copy-start.4 = (f32[2,64,768]{2,1,0:T(8,128)S(1)}, f32[2,64,768]{2,1,0:T(8,128)}, u32[]{:S(2)}) copy-start(f32[2,64,768]{2,1,0:T(8,128)} %param.7) | copy-start | bytes 1179652
  12.0 156.6 %reduce-scatter.2.cloned.1.call-start = ((), (), s32[]{:S(2)}) async-start(), calls=%async_computation.2 | async-start | bytes 1966080 | tf_op jit(solution)/shard_map/reduce_scatter | solution.py:33
  140.5 103.4 %all-reduce.3.cloned.1.call-start = ((), (), s32[]{:S(2)}) async-start(), calls=%async_computation.3 | async-start | bytes 786432 | tf_op jit(solution)/shard_map/psum | solution.py:34
  168.7 132.8 %all-gather.5.cloned.1.call-start = ((), (), s32[]{:S(2)}) async-start(), calls=%async_computation.4 | async-start | bytes 1966080 | tf_op jit(solution)/shard_map/all_gather | solution.py:37
  243.9 37.5 %copy-start.2 = (f32[2,64,768]{2,1,0:T(8,128)S(1)}, f32[2,64,768]{2,1,0:T(8,128)}, u32[]{:S(2)}) copy-start(f32[2,64,768]{2,1,0:T(8,128)} %all-reduce.3.cloned.1.call-done) | copy-start | bytes 1179652
  282.6 106.0 %all-reduce.5.cloned.1.call-start = ((), (), s32[]{:S(2)}) async-start(), calls=%async_computation.5 | async-start | bytes 393216 | tf_op jit(solution)/shard_map/psum | solution.py:39
  388.6 20.9 %copy-start.3 = (bf16[2,64,768]{2,1,0:T(8,128)(2,1)S(1)}, bf16[2,64,768]{2,1,0:T(8,128)(2,1)}, u32[]{:S(2)}) copy-start(bf16[2,64,768]{2,1,0:T(8,128)(2,1)} %all-reduce.5.cloned.1.call-done) | copy-start | bytes 589828
  388.6 24.0 %copy-start.1 = (bf16[2,1024,768]{2,1,0:T(8,128)(2,1)S(1)}, bf16[2,1024,768]{2,1,0:T(8,128)(2,1)}, u32[]{:S(2)}) copy-start(bf16[2,1024,768]{2,1,0:T(8,128)(2,1)} %param.4) | copy-start | bytes 9437188
Sparse Core Ops, SparseCore 0:
  12.2 86.4 all-gather.2
  140.6 27.9 reduce-scatter.1
  172.0 71.8 all-reduce.2
  282.8 18.6 all-gather.4
  317.9 70.6 all-reduce.4
where the time goes:
time: 419 us
  waiting for transfers between devices  279 us (67%)
  matrix products  85 us (20%)
  other arithmetic  22 us (5%)
  between operations  13.9 us (3%)
  blocking collectives  10.9 us (3%)
  local copies, waits for them, and re-layouts  7.81 us (2%)
    all_gather x1, waiting for transfers between devices, compress(): lax.all_gather(out_grad, 'tensor', axis=1, tiled=True)  86.6 us
    psum x1, waiting for transfers between devices, compress(): left_part = lax.psum(left_part, 'dp')  75 us
    psum x1, waiting for transfers between devices, compress(): lax.psum(right_terms.astype(jnp.bfloat16), 'dp').astype(jnp.float32)  70.8 us
    reduce_scatter x1, waiting for transfers between devices, compress(): lax.psum_scatter(left_factor, 'tensor', scatter_dimension=2, tiled=True)  28.1 us
    dot_general x1, matrix products, compress(): jnp.einsum('lre,lde->lrd', right_init, moment, precision=lax.Precision.HI...  22.5 us
    dot_general x1, matrix products, compress(): jnp.einsum('lrd,lre->lde', ortho_basis, right_factor / replicas, precisio...  20.9 us
    dot_general x1, matrix products, compress(): jnp.einsum('ltd,lte->lde', lax.all_gather(out_grad, 'tensor', axis=1, til...  19.3 us
    all_gather x1, waiting for transfers between devices, compress(): ortho_basis = lax.all_gather(ortho_part, 'tensor', axis=2, tiled=True)  18.8 us
  transfers between devices with their start and end apart: 5, of which 5 were waited for; matrix products, arithmetic and copies ran while one was open for 0% of the time, Pallas kernels for 0%

commit v1 on v0

--- a/solution.py
+++ b/solution.py
@@ -2,6 +2,12 @@
 import jax.numpy as jnp
 from jax import lax
 from jax.sharding import PartitionSpec as P
+
+
+def all_parts(block, axis, dim):
+    parts = lax.all_gather(block, axis, axis=0, tiled=False)
+    out = jnp.concatenate(parts, axis=dim)
+    return out
 
 
 def solve_rows(gram_matrix, left_factor):
@@ -24,7 +30,7 @@
     out_width = out_grad.shape[2]
     moment = jnp.einsum(
         "ltd,lte->lde",
-        lax.all_gather(out_grad, "tensor", axis=1, tiled=True),
+        all_parts(out_grad, "tensor", 1),
         context,
         preferred_element_type=jnp.float32,
     )

time: 419 us -> 458 us (1.093)
  local copies, waits for them, and re-layouts: 7.81 us -> 43.9 us
    reshape x0 -> x1, local copies, waits for them, and re-layouts: none -> 20.8 us  [all_parts(): out = jnp.concatenate(parts, axis=dim)]
    all_gather x0 -> x1, local copies, waits for them, and re-layouts: none -> 20.1 us  [all_parts(): parts = lax.all_gather(block, axis, axis=0, tiled=False)]
    unnamed x11 -> x8, local copies, waits for them, and re-layouts: 4.83 us -> 0.03 us
where the time goes in v1:
time: 458 us; the launch traced here: 457 us
  waiting for transfers between devices  280 us (61%)
  matrix products  85.9 us (19%)
  local copies, waits for them, and re-layouts  43.9 us (10%)
  other arithmetic  22 us (5%)
  between operations  13.9 us (3%)
  blocking collectives  10.9 us (2%)
    all_gather x1, waiting for transfers between devices, all_parts(): parts = lax.all_gather(block, axis, axis=0, tiled=False)  86.4 us
    psum x1, waiting for transfers between devices, compress(): left_part = lax.psum(left_part, 'dp')  74.9 us
    psum x1, waiting for transfers between devices, compress(): lax.psum(right_terms.astype(jnp.bfloat16), 'dp').astype(jnp.float32)  70.8 us
    reduce_scatter x1, waiting for transfers between devices, compress(): lax.psum_scatter(left_factor, 'tensor', scatter_dimension=2, tiled=True)  28.1 us
    dot_general x1, matrix products, compress(): jnp.einsum('lre,lde->lrd', right_init, moment, precision=lax.Precision.HI...  22.5 us
    reshape x1, local copies, waits for them, and re-layouts, all_parts(): out = jnp.concatenate(parts, axis=dim)  20.8 us
    dot_general x1, matrix products, compress(): jnp.einsum('lrd,lre->lde', ortho_basis, right_factor / replicas, precisio...  20.8 us
    all_gather x1, local copies, waits for them, and re-layouts, all_parts(): parts = lax.all_gather(block, axis, axis=0, tiled=False)  20.1 us
  transfers between devices with their start and end apart: 5, of which 5 were waited for; matrix products, arithmetic and copies ran while one was open for 0% of the time, Pallas kernels for 0%

profile of v1, /device:TPU:0, one launch (start us, length us, event | category | flops | bytes accessed | tf_op | source)
XLA Modules:
  0.0 456.6 jit_solution(11815629552688774967)
XLA Ops:
  7.2 0.7 all-gather.6.cloned.1.call-update
  8.0 86.4 %all-gather.6.cloned.1.call-done = bf16[8,256,3072]{2,1,0:T(8,128)(2,1)} async-done(((bf16[2,256,3072]{2,1,0:T(8,128)(2,1)}), bf16[8,256,3072]{2,1,0:T(8,128)(2,1)}) %all-gather.6.cloned.1.call-update) | async-done | bytes 12582928 | tf_op jit(solution)/shard_map/all_gather | solution.py:8
  94.4 20.1 %copy.18 = bf16[4,2,256,3072]{2,0,3,1:T(4,128)(2,1)} copy(bf16[4,2,256,3072]{3,2,1,0:T(8,128)(2,1)} %bitcast.29) | data formatting | bytes 25165824 | tf_op jit(solution)/shard_map/all_gather | solution.py:8
  114.5 20.8 %reshape.33 = bf16[2,1024,3072]{1,2,0:T(8,128)(2,1)} reshape(bf16[2,4,256,3072]{2,1,3,0:T(4,128)(2,1)} %bitcast.28) | data formatting | bytes 25165824 | tf_op jit(solution)/shard_map/reshape | solution.py:9
  135.3 19.3 %convert_add_fusion = f32[2,3072,768]{2,1,0:T(8,128)} fusion(bf16[2,3072,768]{2,1,0:T(8,128)(2,1)} %param.6, bf16[2,1024,3072]{1,2,0:T(8,128)(2,1)} %reshape.33, bf16[2,1024,768]{2,1,0:T(8,128)(2,1)S(1)} %copy-done), kind=kOutput, calls=%fused_computation.2 | convolution fusion | flops 9673113600 | bytes 44040192 | tf_op jit(solution)/shard_map/ltd,lte->lde/dot_general | solution.py:31
  154.6 22.5 %convolution_bitcast_fusion = f32[2,64,3072]{2,1,0:T(8,128)} fusion(f32[2,3072,768]{2,1,0:T(8,128)} %convert_add_fusion, f32[2,64,768]{2,1,0:T(8,128)S(1)} %copy-done.3), kind=kOutput, calls=%fused_computation.3 | convolution fusion | flops 3623878656 | bytes 20840448 | tf_op jit(solution)/shard_map/lre,lde->lrd/dot_general | solution.py:38
  177.2 28.1 %reduce-scatter.2.cloned.1.call-done = f32[2,64,768]{2,1,0:T(8,128)} async-done(((f32[2,64,3072]{2,1,0:T(8,128)}), f32[2,64,768]{2,1,0:T(8,128)}) %reduce-scatter.2.cloned.1.call-update) | async-done | bytes 393232 | tf_op jit(solution)/shard_map/reduce_scatter | solution.py:39
  205.5 74.9 %all-reduce.3.cloned.1.call-done = f32[2,64,768]{2,1,0:T(8,128)} async-done(((f32[2,64,768]{2,1,0:T(8,128)}), f32[2,64,768]{2,1,0:T(8,128)}) %all-reduce.3.cloned.1.call-update) | async-done | bytes 393232 | tf_op jit(solution)/shard_map/psum | solution.py:40
  280.4 1.6 fusion.10
  282.1 10.9 %psum.22 = f32[2,64,64]{1,2,0:T(8,128)S(1)} all-reduce(f32[2,64,64]{1,2,0:T(8,128)S(1)} %fusion.10), channel_id=1, replica_groups=mesh['dp'=8,'tensor'=4] {'tensor'}, use_global_device_ids=true, to_apply=%region_2.0 | all-reduce | flops 8192 | bytes 65536 | tf_op jit(solution)/shard_map/psum | solution.py:41
  292.9 1.9 copy.20
  294.9 0.9 gather_fusion
  295.9 0.1 copy.22
  296.0 0.1 fusion.6
  296.1 11.7 %custom-call.8 = f32[2,64,64]{2,1,0:T(8,128)S(1)} custom-call(f32[2,64,64]{2,1,0:T(8,128)S(1)} %fusion.6), custom_call_target="Cholesky" | custom-call | tf_op jit(solution)/shard_map/jit(cholesky)/cholesky | solution.py:17
  307.8 0.1 compare_reduce_fusion
  308.0 0.1 select_bitcast_fusion
  308.0 9.8 %custom-call.9 = f32[2,1,64,64]{2,3,1,0:T(8,128)S(1)} custom-call(f32[2,1,64,64]{3,2,1,0:T(8,128)S(1)} %select_bitcast_fusion), custom_call_target="InvertDiagBlocksLowerTriangular" | custom-call | tf_op jit(solution)/shard_map/vmap(jit(_solve_triangular))/triangular_solve | solution.py:20
  317.9 2.3 fusion.4
  320.2 18.8 %all-gather.4.cloned.1.call-done = f32[2,64,3072]{2,1,0:T(8,128)} async-done(((f32[2,64,768]{2,1,0:T(8,128)}), f32[2,64,3072]{2,1,0:T(8,128)}) %all-gather.4.cloned.1.call-update) | async-done | bytes 1572880 | tf_op jit(solution)/shard_map/all_gather | solution.py:43
  339.0 16.3 %convolution_convert_fusion.1 = bf16[2,64,768]{2,1,0:T(8,128)(2,1)} fusion(f32[2,64,3072]{2,1,0:T(8,128)} %all-gather.4.cloned.1.call-done, f32[2,3072,768]{2,1,0:T(8,128)} %convert_add_fusion), kind=kOutput, calls=%fused_computation.5 | convolution fusion | flops 3623976960 | bytes 20643840 | tf_op jit(solution)/shard_map/lrd,lde->lre/dot_general | solution.py:44
  355.4 70.8 %all-reduce.5.cloned.1.call-done = bf16[2,64,768]{2,1,0:T(8,128)(2,1)} async-done(((bf16[2,64,768]{2,1,0:T(8,128)(2,1)}), bf16[2,64,768]{2,1,0:T(8,128)(2,1)}) %all-reduce.5.cloned.1.call-update) | async-done | bytes 196624 | tf_op jit(solution)/shard_map/psum | solution.py:45
  426.2 20.8 %subtract_convert_fusion = bf16[2,3072,768]{2,1,0:T(8,128)(2,1)} fusion(f32[2,3072,768]{2,1,0:T(8,128)} %convert_add_fusion, f32[2,64,3072]{2,1,0:T(8,128)} %all-gather.4.cloned.1.call-done, bf16[2,64,768]{2,1,0:T(8,128)(2,1)} %all-reduce.5.cloned.1.call-done), kind=kOutput, calls=%fused_computation.1 | convolution fusion | flops 3633512448 | bytes 30081024 | tf_op jit(solution)/shard_map/lrd,lre->lde/dot_general | solution.py:52
  446.9 3.1 convolution_convert_fusion
  (26 shorter events, 0.5 us)
Async XLA Ops:
  7.2 128.1 %copy-start = (bf16[2,1024,768]{2,1,0:T(8,128)(2,1)S(1)}, bf16[2,1024,768]{2,1,0:T(8,128)(2,1)}, u32[]{:S(2)}) copy-start(bf16[2,1024,768]{2,1,0:T(8,128)(2,1)} %param.4) | copy-start | bytes 9437188
  7.2 87.2 %all-gather.6.cloned.1.call-start = ((), (), s32[]{:S(2)}) async-start(), calls=%async_computation.5 | async-start | bytes 15728640 | tf_op jit(solution)/shard_map/all_gather | solution.py:8
  7.9 197.4 %reduce-scatter.2.cloned.1.call-start = ((), (), s32[]{:S(2)}) async-start(), calls=%async_computation.1 | async-start | bytes 1966080 | tf_op jit(solution)/shard_map/reduce_scatter | solution.py:39
  135.3 19.3 %copy-start.3 = (f32[2,64,768]{2,1,0:T(8,128)S(1)}, f32[2,64,768]{2,1,0:T(8,128)}, u32[]{:S(2)}) copy-start(f32[2,64,768]{2,1,0:T(8,128)} %param.7) | copy-start | bytes 1179652
  177.1 103.3 %all-reduce.3.cloned.1.call-start = ((), (), s32[]{:S(2)}) async-start(), calls=%async_computation.2 | async-start | bytes 786432 | tf_op jit(solution)/shard_map/psum | solution.py:40
  205.3 133.7 %all-gather.4.cloned.1.call-start = ((), (), s32[]{:S(2)}) async-start(), calls=%async_computation.3 | async-start | bytes 1966080 | tf_op jit(solution)/shard_map/all_gather | solution.py:43
  320.2 106.0 %all-reduce.5.cloned.1.call-start = ((), (), s32[]{:S(2)}) async-start(), calls=%async_computation.4 | async-start | bytes 393216 | tf_op jit(solution)/shard_map/psum | solution.py:45
  355.3 94.7 %copy-start.1 = (bf16[2,1024,768]{2,1,0:T(8,128)(2,1)S(1)}, bf16[2,1024,768]{2,1,0:T(8,128)(2,1)}, u32[]{:S(2)}) copy-start(bf16[2,1024,768]{2,1,0:T(8,128)(2,1)} %param.4) | copy-start | bytes 9437188
  426.2 20.8 %copy-start.2 = (bf16[2,64,768]{2,1,0:T(8,128)(2,1)S(1)}, bf16[2,64,768]{2,1,0:T(8,128)(2,1)}, u32[]{:S(2)}) copy-start(bf16[2,64,768]{2,1,0:T(8,128)(2,1)} %all-reduce.5.cloned.1.call-done) | copy-start | bytes 589828
Sparse Core Ops, SparseCore 0:
  9.5 84.7 all-gather.5
  177.3 27.9 reduce-scatter.1
  208.6 71.7 all-reduce.2
  320.3 18.6 all-gather.3
  355.5 70.6 all-reduce.4
